TPU v7x, 32 devices: a whole 2x2x4 slice. The times are simulated.
32 devices in a mesh: mode: 16 (over z, y, x), real: 2 (over core).
Axes of the slice: x: 2, y: 2, z: 4, core: 2. Of those that a mesh axis runs over, the one named last changes fastest.
Arguments:
- input_field: bfloat16 [2, 2, 256, 16384], P(None, 'real', 'mode'), may hold values from -6 to 6
- kerr_coeff: bfloat16 [16, 64, 64], P('mode'), may hold values from -0.375 to 0.375
- block_list: int32 [16, 4], P('mode'), may hold values from 0 to 31
Outputs:
- density: float32 [512, 2, 256, 256], P('mode', None, 'real')
All inputs are finite; a program needn't handle non-finite values.
Results may differ from a plain program's by a relative error of at most 0.0085.
Values may be sent and summed in bfloat16 or wider, within the bound.
A program may use at most 64 MiB of HBM per device.

v0:
```python
import math
import jax
import jax.numpy as jnp
from jax import lax
from jax.sharding import PartitionSpec as P

MB = 8
FT = 128
NT = 16384
FB = 32
kerr_strength = 0.25


def kerr_terms(field_blocks, coeff_group, block_group):
    mode_l = jnp.take(field_blocks, block_group[:, 1], axis=2).astype(jnp.float32)
    mode_m = jnp.take(field_blocks, block_group[:, 2], axis=2).astype(jnp.float32)
    mode_n = jnp.take(field_blocks, block_group[:, 3], axis=2).astype(jnp.float32)
    realiz = field_blocks.shape[1]
    group_size = block_group.shape[0]
    steps_local = field_blocks.shape[4]
    prod_re = (
        mode_m[0][:, :, :, None, :] * mode_n[0][:, :, None, :, :]
        + mode_m[1][:, :, :, None, :] * mode_n[1][:, :, None, :, :]
    )
    prod_im = (
        mode_m[1][:, :, :, None, :] * mode_n[0][:, :, None, :, :]
        - mode_m[0][:, :, :, None, :] * mode_n[1][:, :, None, :, :]
    )
    pairs = (
        jnp.stack([prod_re, prod_im])
        .reshape(2, realiz, group_size, MB * MB, steps_local)
        .astype(jnp.bfloat16)
    )
    weighted = jnp.einsum(
        "kab,crkbt->crkat", coeff_group, pairs, preferred_element_type=jnp.float32
    )
    weighted = weighted.reshape(2, realiz, group_size, MB, MB, steps_local)
    term_re = jnp.sum(
        weighted[0] * mode_l[0][:, :, None] - weighted[1] * mode_l[1][:, :, None], axis=3
    )
    term_im = jnp.sum(
        weighted[0] * mode_l[1][:, :, None] + weighted[1] * mode_l[0][:, :, None], axis=3
    )
    one_hot = (
        block_group[:, 0][:, None] == jnp.arange(field_blocks.shape[2], dtype=jnp.int32)[None, :]
    ).astype(jnp.float32)
    return jnp.einsum(
        "kg,crkpt->crgpt", one_hot, jnp.stack([term_re, term_im]), precision=lax.Precision.HIGHEST
    )


def phase_table(extent, modulus):
    index_a = jnp.arange(extent, dtype=jnp.int32)[:, None]
    index_b = jnp.arange(extent, dtype=jnp.int32)[None, :]
    angle = 2.0 * math.pi / modulus * (index_a * index_b % modulus).astype(jnp.float32)
    return (jnp.cos(angle), -jnp.sin(angle))


def first_pass(table, data):
    table_high = table.astype(jnp.bfloat16)
    table_low = (table - table_high.astype(jnp.float32)).astype(jnp.bfloat16)
    upper = jnp.einsum("kn,rmnj->rmkj", table_high, data, preferred_element_type=jnp.float32)
    return upper + jnp.einsum("kn,rmnj->rmkj", table_low, data, preferred_element_type=jnp.float32)


def second_pass(table, data):
    return jnp.einsum("jn,rmkn->rmjk", table, data, precision=lax.Precision.HIGH)


def transform(by_mode):
    realiz = by_mode.shape[1]
    local_modes = by_mode.shape[2]
    signal = by_mode.reshape(2, realiz, local_modes, FT, FT)
    four_re, four_im = phase_table(FT, FT)
    twist_re, twist_im = phase_table(FT, NT)
    half_re = first_pass(four_re, signal[0]) - first_pass(four_im, signal[1])
    half_im = first_pass(four_re, signal[1]) + first_pass(four_im, signal[0])
    turned_re = half_re * twist_re - half_im * twist_im
    turned_im = half_re * twist_im + half_im * twist_re
    out_re = (second_pass(four_re, turned_re) - second_pass(four_im, turned_im)) / FT
    out_im = (second_pass(four_re, turned_im) + second_pass(four_im, turned_re)) / FT
    return jnp.stack([out_re, out_im]).astype(jnp.bfloat16)


def gram_parts(rows_part, cols_part):
    quarters = jnp.einsum(
        "crpbf,drqbf->bcdpq", rows_part, cols_part, preferred_element_type=jnp.float32
    )
    return jnp.stack(
        [quarters[:, 0, 0] + quarters[:, 1, 1], quarters[:, 1, 0] - quarters[:, 0, 1]], axis=1
    )


def shards(input_field, kerr_coeff, block_list):
    timed = lax.all_to_all(input_field, "mode", split_axis=3, concat_axis=2, tiled=True)
    realiz = timed.shape[1]
    width = timed.shape[2]
    steps_local = timed.shape[3]
    field_blocks = timed.reshape(2, realiz, width // MB, MB, steps_local)
    initial = jnp.zeros(field_blocks.shape, jnp.float32)
    running = initial
    coeff_piece = lax.all_gather(kerr_coeff, "mode", axis=0, tiled=True)
    block_piece = lax.all_gather(block_list, "mode", axis=0, tiled=True)
    block_count = block_piece.shape[0]
    coeff_groups = coeff_piece.reshape(
        block_count // 8, 8, coeff_piece.shape[1], coeff_piece.shape[2]
    )
    block_groups = block_piece.reshape(block_count // 8, 8, 4)

    def one_group(carried, groups):
        return (carried + kerr_terms(field_blocks, groups[0], groups[1]), None)

    running, unused = lax.scan(one_group, running, (coeff_groups, block_groups))
    kerr_sum = running
    kerr_sum = kerr_sum.reshape(2, realiz, width, steps_local)
    base = timed.astype(jnp.float32)
    stepped = jnp.stack(
        [base[0] - kerr_strength * kerr_sum[1], base[1] + kerr_strength * kerr_sum[0]]
    ).astype(jnp.bfloat16)
    by_mode = lax.all_to_all(stepped, "mode", split_axis=2, concat_axis=3, tiled=True)
    spectrum = transform(by_mode)
    banded = lax.all_to_all(spectrum, "mode", split_axis=3, concat_axis=2, tiled=True)
    bands_dev = banded.shape[3] * FT // FB
    spec_bands = banded.reshape(2, realiz, width, bands_dev, FB)
    scale = 1.0 / (FB * realiz * lax.axis_size("real"))
    row_count = width // lax.axis_size("real")
    row_first = lax.axis_index("real") * row_count
    shard_piece = lax.all_gather(spec_bands, "real", axis=1, tiled=True)
    own_part = lax.dynamic_slice_in_dim(shard_piece, row_first, row_count, 2)
    return gram_parts(own_part, shard_piece) * scale


def solution(mesh):
    return jax.shard_map(
        shards,
        mesh=mesh,
        in_specs=(P(None, "real", "mode", None), P("mode", None, None), P("mode", None)),
        out_specs=P("mode", None, "real", None),
        check_vma=False,
    )
```

profile of v0, /device:TPU:0, one launch (start us, length us, event | category | flops | bytes accessed | tf_op | source)
XLA Modules:
  0.0 297.2 jit_solution(920240638021889750)
XLA Ops:
  6.5 15.9 %copy.145 = bf16[2,1,16,16384]{2,0,1,3:T(2,128)(2,1)} copy(bf16[2,1,16,16384]{3,2,1,0:T(8,128)(2,1)} %param.7) | data formatting | bytes 2097152 | tf_op args[0]
  22.5 11.2 %reshape.574 = bf16[16,2,16384]{2,1,0:T(2,128)(2,1)} reshape(bf16[16384,1,2,16]{3,2,1,0:T(2,128)(2,1)} %bitcast.267) | data formatting | bytes 2097152
  33.7 8.5 %all-to-all-start = ((bf16[16,2,16384]{2,1,0:T(2,128)(2,1)}), bf16[16,2,16384]{2,1,0:T(2,128)(2,1)S(1)}, u32[]{:S(2)}, u32[]{:S(2)}) async-start(bf16[16,2,16384]{2,1,0:T(2,128)(2,1)} %reshape.574), calls=%async_computation | async-start | bytes 2097152 | tf_op jit(solution)/shard_map/all_to_all | solution.py:95
  42.2 50.9 %all-gather = s32[16,1,4]{2,1,0:T(1,128)S(1)} all-gather(s32[1,1,4]{2,1,0:T(1,128)S(1)} %bitcast.278), channel_id=1, replica_groups=mesh['mode'=16,'real'=2] {'mode'}, dimensions={0}, use_global_device_ids=true | all-gather | bytes 272 | tf_op jit(solution)/shard_map/all_gather | solution.py:103
  93.2 38.7 %all_gather.10 = bf16[16,64,64]{2,1,0:T(8,128)(2,1)S(1)} all-gather(bf16[1,64,64]{2,1,0:T(8,128)(2,1)S(1)} %copy-done.4), channel_id=1, replica_groups=mesh['mode'=16,'real'=2] {'mode'}, dimensions={0}, use_global_device_ids=true | all-gather | bytes 139264 | tf_op jit(solution)/shard_map/all_gather | solution.py:102
  131.8 7.4 %reshape.575 = bf16[16384,1,2,16]{3,2,1,0:T(2,128)(2,1)} reshape(bf16[16,2,16384]{2,1,0:T(2,128)(2,1)S(1)} %all-to-all-done) | data formatting | bytes 2097152
  139.2 17.7 %copy.200 = bf16[2,1,16,16,1024]{4,2,3,0,1:T(8,128)(2,1)S(1)} copy(bf16[2,1,16,16,1024]{2,0,4,3,1:T(2,128)(2,1)} %bitcast.265) | data formatting | bytes 2097152 | tf_op jit(solution)/shard_map/all_to_all | solution.py:95
  156.9 12.7 %copy.197 = bf16[2,1,16,16,1024]{4,3,2,0,1:T(8,128)(2,1)} copy(bf16[2,1,16,16,1024]{2,0,4,3,1:T(2,128)(2,1)} %bitcast.266) | data formatting | bytes 2097152 | tf_op jit(solution)/shard_map/all_to_all | solution.py:95
  169.6 23.4 %while.11 = (s32[]{:T(128)}, f32[2,1,32,8,1024]{4,2,3,0,1:T(8,128)S(1)}, s32[2,8,4]{1,2,0:T(4,128)S(1)}, bf16[2,1,32,8,1024]{4,3,2,1,0:T(8,128)(2,1)S(1)}, bf16[...) while((s32[]{:T(128)}, f32[2,1,32,8,1024]{4,2,3,0,1:T(8,128)S(1)}, ...), condition=%wide.region_3.5_spmd.clone, body=%wide.region_0.4_spmd.clone.sunk | while | flops 198970768 | bytes 36058028 | solution.py:113
  169.7 0.9 copy-done
  170.6 1.8 gather_fusion.2
  172.4 1.8 gather_fusion.1
  174.2 1.8 gather_fusion
  176.4 0.6 fusion.157
  177.0 0.7 convolution_bitcast_fusion.3
  177.7 1.5 subtract_reduce_fusion.2
  179.6 1.7 bitcast_add_fusion.2
  181.4 0.9 copy-done
  182.3 1.8 gather_fusion.2
  184.1 1.8 gather_fusion.1
  185.9 1.8 gather_fusion
  188.1 0.6 fusion.157
  188.8 0.7 convolution_bitcast_fusion.3
  189.5 1.5 subtract_reduce_fusion.2
  191.4 1.7 bitcast_add_fusion.2
  193.1 1.2 copy.152
  194.8 0.6 copy.147
  195.4 0.6 copy.153
  196.7 2.0 copy.155
  198.7 3.7 %all-to-all-start.1 = ((bf16[2,1,256,1024]{3,0,1,2:T(2,128)(2,1)}), bf16[2,1,256,1024]{3,0,1,2:T(2,128)(2,1)S(1)}, u32[]{:S(2)}, u32[]{:S(2)}) async-start(bf16[2,1,256,1024]{3,0,1,2:T(2,128)(2,1)} %copy.155), calls=%async_computation.1 | async-start | bytes 2097152 | tf_op jit(solution)/shard_map/all_to_all | solution.py:120
  203.3 14.6 %all-to-all-done.1 = bf16[2,1,256,1024]{3,0,1,2:T(2,128)(2,1)S(1)} async-done(((bf16[2,1,256,1024]{3,0,1,2:T(2,128)(2,1)}), bf16[2,1,256,1024]{3,0,1,2:T(2,128)(2,1)S(1)}, u32[]{:S(2)}, u32[]{:S(2)}) %all-to-all-start.1) | async-done | bytes 1048608 | tf_op jit(solution)/shard_map/all_to_all | solution.py:120
  218.2 0.9 fusion.137
  220.7 1.1 copy.157
  221.8 1.3 reshape.509
  226.4 1.2 fusion.39
  227.6 1.2 fusion.43
  228.8 1.2 fusion.30
  229.9 1.2 fusion.31
  231.2 1.0 copy.173
  232.2 21.6 %all_to_all.45 = bf16[2,1,16,128,128]{4,2,1,0,3:T(8,128)(2,1)S(1)} all-to-all(bf16[2,1,16,128,128]{4,2,1,0,3:T(8,128)(2,1)S(1)} %copy.173), channel_id=1, replica_groups=mesh['mode'=16,'real'=2] {'mode'}, dimensions={3} | all-to-all | bytes 2097152 | tf_op jit(solution)/shard_map/all_to_all | solution.py:122
  254.5 3.2 %reshape.513 = bf16[2,1,256,32,32]{4,3,2,0,1:T(8,128)(2,1)} reshape(bf16[2,1,16,16,8,128]{5,4,3,2,0,1:T(8,128)(2,1)S(1)} %copy.175) | data formatting | bytes 2097152 | tf_op jit(solution)/shard_map/reshape | solution.py:124
  257.7 5.2 %copy.176 = bf16[2,1,256,32,32]{2,4,1,0,3:T(8,128)(2,1)} copy(bf16[2,1,256,32,32]{4,3,2,0,1:T(8,128)(2,1)} %reshape.513) | data formatting | bytes 2097152 | tf_op jit(solution)/shard_map/reshape | solution.py:124
  263.0 9.0 %all-gather.3.cloned.1.call-done = bf16[2,2,256,32,32]{2,4,1,0,3:T(8,128)(2,1)} async-done(((bf16[2,1,256,32,32]{2,4,1,0,3:T(8,128)(2,1)}), bf16[2,2,256,32,32]{2,4,1,0,3:T(8,128)(2,1)}) %all-gather.3.cloned.1.call-update) | async-done | bytes 2097168 | tf_op jit(solution)/shard_map/all_gather | solution.py:128
  272.0 4.2 %convolution_bitcast_fusion.1 = f32[32,2,2,128,256]{3,4,1,2,0:T(8,128)S(1)} fusion(bf16[2,2,256,32,32]{2,4,1,0,3:T(8,128)(2,1)} %all-gather.3.cloned.1.call-done, s32[]{:T(128)S(6)} %select_n.66), kind=kOutput, calls=%fused_computation.52 | convolution fusion | flops 536870912 | bytes 19922948 | tf_op jit(solution)/shard_map/crpbf,drqbf->bcdpq/dot_general | solution.py:86
  276.2 0.6 fusion.18
  276.9 0.6 fusion.20
  277.5 3.9 %maximum_multiply_fusion = f32[32,2,128,256]{2,3,0,1:T(8,128)} fusion(f32[32,1,128,256]{2,3,0,1:T(8,128)S(1)} %fusion.18, f32[32,1,128,256]{2,3,0,1:T(8,128)S(1)} %fusion.20), kind=kLoop, calls=%fused_computation.53 | loop fusion | flops 4194304 | bytes 16777216 | tf_op jit(solution)/shard_map/mul | solution.py:130
  281.4 8.9 %copy.179 = f32[32,2,128,256]{3,2,1,0:T(8,128)} copy(f32[32,2,128,256]{2,3,0,1:T(8,128)} %maximum_multiply_fusion) | data formatting | bytes 16777216 | tf_op jit(solution)/shard_map/mul | solution.py:130
  (67 shorter events, 9.4 us)
Async XLA Ops:
  33.7 8.5 %copy-start.5 = (s32[1,4]{1,0:T(1,128)S(1)}, s32[1,4]{1,0:T(1,128)}, u32[]{:S(2)}) copy-start(s32[1,4]{1,0:T(1,128)} %param.9) | copy-start | bytes 52
  33.7 59.5 %copy-start.4 = (bf16[1,64,64]{2,1,0:T(8,128)(2,1)S(1)}, bf16[1,64,64]{2,1,0:T(8,128)(2,1)}, u32[]{:S(2)}) copy-start(bf16[1,64,64]{2,1,0:T(8,128)(2,1)} %param.8) | copy-start | bytes 24580
  33.7 98.1 %all-to-all-start = ((bf16[16,2,16384]{2,1,0:T(2,128)(2,1)}), bf16[16,2,16384]{2,1,0:T(2,128)(2,1)S(1)}, u32[]{:S(2)}, u32[]{:S(2)}) async-start(bf16[16,2,16384]{2,1,0:T(2,128)(2,1)} %reshape.574), calls=%async_computation | async-start | bytes 2097152 | tf_op jit(solution)/shard_map/all_to_all | solution.py:95
  169.6 1.0 copy-start
  179.6 1.7 copy-start.1
  181.4 1.0 copy-start
  191.3 1.7 copy-start.1
  193.1 1.2 copy-start.2
  198.7 19.2 %all-to-all-start.1 = ((bf16[2,1,256,1024]{3,0,1,2:T(2,128)(2,1)}), bf16[2,1,256,1024]{3,0,1,2:T(2,128)(2,1)S(1)}, u32[]{:S(2)}, u32[]{:S(2)}) async-start(bf16[2,1,256,1024]{3,0,1,2:T(2,128)(2,1)} %copy.155), calls=%async_computation.1 | async-start | bytes 2097152 | tf_op jit(solution)/shard_map/all_to_all | solution.py:120
  202.4 69.6 %all-gather.3.cloned.1.call-start = ((), (), s32[]{:S(2)}) async-start(), calls=%async_computation.3 | async-start | bytes 3145728 | tf_op jit(solution)/shard_map/all_gather | solution.py:128
  219.6 1.1 copy-start.3
Sparse Core Ops, SparseCore 0:
  263.1 8.8 all-gather.2
where the time goes:
time: 300 us; the launch traced here: 297 us
  blocking collectives  111 us (37%)
  local copies, waits for them, and re-layouts  106 us (35%)
  waiting for transfers between devices  23.6 us (8%)
  matrix products  18.1 us (6%)
  between operations  13.7 us (5%)
  starting transfers between devices  12.3 us (4%)
  other arithmetic  11.5 us (4%)
    all_gather x1, blocking collectives, shards(): block_piece = lax.all_gather(block_list, 'mode', axis=0, tiled=True)  50.9 us
    all_gather x1, blocking collectives, shards(): coeff_piece = lax.all_gather(kerr_coeff, 'mode', axis=0, tiled=True)  38.7 us
    unnamed x12, local copies, waits for them, and re-layouts  34.7 us
    all_to_all x2, local copies, waits for them, and re-layouts, shards(): lax.all_to_all(input_field, 'mode', split_axis=3, concat_axis=2, tiled=True)  30.4 us
    all_to_all x1, blocking collectives, shards(): lax.all_to_all(spectrum, 'mode', split_axis=3, concat_axis=2, tiled=True)  21.6 us
    all_to_all x1, waiting for transfers between devices, shards(): lax.all_to_all(stepped, 'mode', split_axis=2, concat_axis=3, tiled=True)  14.6 us
    all_gather x1, waiting for transfers between devices, shards(): shard_piece = lax.all_gather(spec_bands, 'real', axis=1, tiled=True)  9 us
    mul x1, local copies, waits for them, and re-layouts, shards(): return gram_parts(own_part, shard_piece) * scale  8.94 us
  transfers between devices with their start and end apart: 3, of which 2 were waited for; matrix products, arithmetic and copies ran while one was open for 0% of the time, Pallas kernels for 0%

commit v1 on v0

--- a/solution.py
+++ b/solution.py
@@ -9,6 +9,18 @@
 NT = 16384
 FB = 32
 kerr_strength = 0.25
+
+
+def collect(x, axis, dim):
+    ways, here = (lax.axis_size(axis), lax.axis_index(axis))
+    grown, reach = (x, 1)
+    while reach < ways:
+        theirs = lax.ppermute(grown, axis, [(d, d ^ reach) for d in range(ways)])
+        mine_first = jnp.concatenate([grown, theirs], axis=dim)
+        theirs_first = jnp.concatenate([theirs, grown], axis=dim)
+        grown = jnp.where(here & reach == 0, mine_first, theirs_first)
+        reach = 2 * reach
+    return grown
 
 
 def kerr_terms(field_blocks, coeff_group, block_group):
@@ -100,7 +112,7 @@
     initial = jnp.zeros(field_blocks.shape, jnp.float32)
     running = initial
     coeff_piece = lax.all_gather(kerr_coeff, "mode", axis=0, tiled=True)
-    block_piece = lax.all_gather(block_list, "mode", axis=0, tiled=True)
+    block_piece = collect(block_list, "mode", 0)
     block_count = block_piece.shape[0]
     coeff_groups = coeff_piece.reshape(
         block_count // 8, 8, coeff_piece.shape[1], coeff_piece.shape[2]

time: 300 us -> 275 us (0.917)
  blocking collectives: 111 us -> 72.5 us
  waiting for transfers between devices: 23.6 us -> 34.4 us
    all_gather x1 -> x0, blocking collectives: 50.9 us -> none  [shards(): block_piece = lax.all_gather(block_list, 'mode', axis=0, tiled=True)]
    all_gather x1, blocking collectives: 38.7 us -> 50.7 us  [shards(): coeff_piece = lax.all_gather(kerr_coeff, 'mode', axis=0, tiled=True)]
    ppermute x0 -> x4, waiting for transfers between devices: none -> 10.9 us  [collect(): theirs = lax.ppermute(grown, axis, [(d, d ^ reach) for d in range(ways)])]
  transfers between devices with their start and end apart: 3 -> 7, of which waited for: 2 -> 5; matrix products, arithmetic and copies ran while one was open for 0% -> 0% of each run, Pallas kernels for 0% -> 0%
where the time goes in v1:
time: 275 us; the launch traced here: 271 us
  local copies, waits for them, and re-layouts  104 us (38%)
  blocking collectives  72.5 us (26%)
  waiting for transfers between devices  34.4 us (13%)
  matrix products  19 us (7%)
  starting transfers between devices  15 us (5%)
  between operations  13.7 us (5%)
  other arithmetic  11.8 us (4%)
    all_gather x1, blocking collectives, shards(): coeff_piece = lax.all_gather(kerr_coeff, 'mode', axis=0, tiled=True)  50.7 us
    unnamed x12, local copies, waits for them, and re-layouts  35.3 us
    all_to_all x2, local copies, waits for them, and re-layouts, shards(): lax.all_to_all(input_field, 'mode', split_axis=3, concat_axis=2, tiled=True)  30.4 us
    all_to_all x1, blocking collectives, shards(): lax.all_to_all(spectrum, 'mode', split_axis=3, concat_axis=2, tiled=True)  21.8 us
    all_to_all x1, waiting for transfers between devices, shards(): lax.all_to_all(stepped, 'mode', split_axis=2, concat_axis=3, tiled=True)  14.6 us
    ppermute x4, waiting for transfers between devices, collect(): theirs = lax.ppermute(grown, axis, [(d, d ^ reach) for d in range(ways)])  10.9 us
    all_gather x1, waiting for transfers between devices, shards(): shard_piece = lax.all_gather(spec_bands, 'real', axis=1, tiled=True)  9 us
    mul x1, local copies, waits for them, and re-layouts, shards(): return gram_parts(own_part, shard_piece) * scale  8.94 us
  transfers between devices with their start and end apart: 7, of which 5 were waited for; matrix products, arithmetic and copies ran while one was open for 0% of the time, Pallas kernels for 0%

profile of v1, /device:TPU:0, one launch (start us, length us, event | category | flops | bytes accessed | tf_op | source)
XLA Modules:
  0.0 271.4 jit_solution(5978999099854220259)
XLA Ops:
  6.5 15.9 %copy.151 = bf16[2,1,16,16384]{2,0,1,3:T(2,128)(2,1)} copy(bf16[2,1,16,16384]{3,2,1,0:T(8,128)(2,1)} %param.7) | data formatting | bytes 2097152 | tf_op args[0]
  22.5 11.2 %reshape.572 = bf16[16,2,16384]{2,1,0:T(2,128)(2,1)} reshape(bf16[16384,1,2,16]{3,2,1,0:T(2,128)(2,1)} %bitcast.268) | data formatting | bytes 2097152
  33.7 8.5 %all-to-all-start = ((bf16[16,2,16384]{2,1,0:T(2,128)(2,1)}), bf16[16,2,16384]{2,1,0:T(2,128)(2,1)S(1)}, u32[]{:S(2)}, u32[]{:S(2)}) async-start(bf16[16,2,16384]{2,1,0:T(2,128)(2,1)} %reshape.572), calls=%async_computation | async-start | bytes 2097152 | tf_op jit(solution)/shard_map/all_to_all | solution.py:107
  42.3 1.9 collective-permute-start
  44.2 50.7 %all_gather.6 = bf16[16,64,64]{2,1,0:T(8,128)(2,1)S(1)} all-gather(bf16[1,64,64]{2,1,0:T(8,128)(2,1)S(1)} %copy-done.4), channel_id=1, replica_groups=mesh['mode'=16,'real'=2] {'mode'}, dimensions={0}, use_global_device_ids=true | all-gather | bytes 139264 | tf_op jit(solution)/shard_map/all_gather | solution.py:114
  95.0 3.6 %collective-permute-done.1 = s32[2,4]{0,1:T(4,128)S(1)} collective-permute-done((s32[2,4]{0,1:T(4,128)S(1)}, s32[2,4]{0,1:T(4,128)S(1)}, u32[]{:S(2)}, u32[]{:S(2)}) %collective-permute-start.1) | collective-permute-done | bytes 64 | tf_op jit(solution)/shard_map/ppermute | solution.py:18
  98.6 3.6 %collective-permute-done.2 = s32[4,4]{0,1:T(4,128)S(1)} collective-permute-done((s32[4,4]{0,1:T(4,128)S(1)}, s32[4,4]{0,1:T(4,128)S(1)}, u32[]{:S(2)}, u32[]{:S(2)}) %collective-permute-start.2) | collective-permute-done | bytes 96 | tf_op jit(solution)/shard_map/ppermute | solution.py:18
  102.3 0.7 collective-permute-start.3
  103.0 3.7 %collective-permute-done.3 = s32[8,4]{0,1:T(4,128)S(1)} collective-permute-done((s32[8,4]{0,1:T(4,128)S(1)}, s32[8,4]{0,1:T(4,128)S(1)}, u32[]{:S(2)}, u32[]{:S(2)}) %collective-permute-start.3) | collective-permute-done | bytes 160 | tf_op jit(solution)/shard_map/ppermute | solution.py:18
  106.9 7.4 %reshape.573 = bf16[16384,1,2,16]{3,2,1,0:T(2,128)(2,1)} reshape(bf16[16,2,16384]{2,1,0:T(2,128)(2,1)S(1)} %all-to-all-done) | data formatting | bytes 2097152
  114.3 17.7 %copy.206 = bf16[2,1,16,16,1024]{4,2,3,0,1:T(8,128)(2,1)S(1)} copy(bf16[2,1,16,16,1024]{2,0,4,3,1:T(2,128)(2,1)} %bitcast.266) | data formatting | bytes 2097152 | tf_op jit(solution)/shard_map/all_to_all | solution.py:107
  132.0 12.7 %copy.205 = bf16[2,1,16,16,1024]{4,3,2,0,1:T(8,128)(2,1)} copy(bf16[2,1,16,16,1024]{2,0,4,3,1:T(2,128)(2,1)} %bitcast.267) | data formatting | bytes 2097152 | tf_op jit(solution)/shard_map/all_to_all | solution.py:107
  144.7 23.4 %while.11 = (s32[]{:T(128)}, f32[2,1,32,8,1024]{4,2,3,0,1:T(8,128)S(1)}, s32[2,8,4]{1,0,2:T(2,128)S(1)}, bf16[2,1,32,8,1024]{4,3,2,1,0:T(8,128)(2,1)S(1)}, bf16[...) while((s32[]{:T(128)}, f32[2,1,32,8,1024]{4,2,3,0,1:T(8,128)S(1)}, ...), condition=%wide.region_3.5_spmd.clone, body=%wide.region_0.4_spmd.clone.sunk | while | flops 198970768 | bytes 36058028 | solution.py:125
  144.8 0.9 copy-done
  145.7 1.8 gather_fusion.2
  147.5 1.8 gather_fusion.1
  149.3 1.8 gather_fusion
  151.5 0.6 fusion.157
  152.1 0.7 convolution_bitcast_fusion.3
  152.8 1.5 subtract_reduce_fusion.2
  154.7 1.7 bitcast_add_fusion.2
  156.5 0.9 copy-done
  157.4 1.8 gather_fusion.2
  159.2 1.8 gather_fusion.1
  161.0 1.8 gather_fusion
  163.8 0.7 convolution_bitcast_fusion.3
  164.5 1.5 subtract_reduce_fusion.2
  166.4 1.7 bitcast_add_fusion.2
  168.2 1.2 copy.160
  171.6 2.0 copy.163
  173.6 3.7 %all-to-all-start.1 = ((bf16[2,1,256,1024]{3,0,1,2:T(2,128)(2,1)}), bf16[2,1,256,1024]{3,0,1,2:T(2,128)(2,1)S(1)}, u32[]{:S(2)}, u32[]{:S(2)}) async-start(bf16[2,1,256,1024]{3,0,1,2:T(2,128)(2,1)} %copy.163), calls=%async_computation.1 | async-start | bytes 2097152 | tf_op jit(solution)/shard_map/all_to_all | solution.py:132
  178.3 14.6 %all-to-all-done.1 = bf16[2,1,256,1024]{3,0,1,2:T(2,128)(2,1)S(1)} async-done(((bf16[2,1,256,1024]{3,0,1,2:T(2,128)(2,1)}), bf16[2,1,256,1024]{3,0,1,2:T(2,128)(2,1)S(1)}, u32[]{:S(2)}, u32[]{:S(2)}) %all-to-all-start.1) | async-done | bytes 1048608 | tf_op jit(solution)/shard_map/all_to_all | solution.py:132
  194.2 1.5 fusion.85
  199.0 0.7 copy-done.3
  200.2 1.2 fusion.39
  201.4 1.2 fusion.43
  202.6 1.2 fusion.30
  203.8 1.2 fusion.31
  205.1 1.0 copy.181
  206.1 21.8 %all_to_all.45 = bf16[2,1,16,128,128]{4,2,1,0,3:T(8,128)(2,1)S(1)} all-to-all(bf16[2,1,16,128,128]{4,2,1,0,3:T(8,128)(2,1)S(1)} %copy.181), channel_id=1, replica_groups=mesh['mode'=16,'real'=2] {'mode'}, dimensions={3} | all-to-all | bytes 2097152 | tf_op jit(solution)/shard_map/all_to_all | solution.py:134
  228.6 3.2 %reshape.514 = bf16[2,1,256,32,32]{4,3,2,0,1:T(8,128)(2,1)} reshape(bf16[2,1,16,16,8,128]{5,4,3,2,0,1:T(8,128)(2,1)S(1)} %copy.183) | data formatting | bytes 2097152 | tf_op jit(solution)/shard_map/reshape | solution.py:136
  231.9 5.2 %copy.184 = bf16[2,1,256,32,32]{2,4,1,0,3:T(8,128)(2,1)} copy(bf16[2,1,256,32,32]{4,3,2,0,1:T(8,128)(2,1)} %reshape.514) | data formatting | bytes 2097152 | tf_op jit(solution)/shard_map/reshape | solution.py:136
  237.1 9.0 %all-gather.2.cloned.1.call-done = bf16[2,2,256,32,32]{2,4,1,0,3:T(8,128)(2,1)} async-done(((bf16[2,1,256,32,32]{2,4,1,0,3:T(8,128)(2,1)}), bf16[2,2,256,32,32]{2,4,1,0,3:T(8,128)(2,1)}) %all-gather.2.cloned.1.call-update) | async-done | bytes 2097168 | tf_op jit(solution)/shard_map/all_gather | solution.py:140
  246.1 4.2 %convolution_bitcast_fusion.1 = f32[32,2,2,128,256]{3,4,1,2,0:T(8,128)S(1)} fusion(bf16[2,2,256,32,32]{2,4,1,0,3:T(8,128)(2,1)} %all-gather.2.cloned.1.call-done, s32[]{:T(128)S(6)} %select_n.111), kind=kOutput, calls=%fused_computation.52 | convolution fusion | flops 536870912 | bytes 19922948 | tf_op jit(solution)/shard_map/crpbf,drqbf->bcdpq/dot_general | solution.py:98
  250.4 0.6 fusion.18
  251.0 0.6 fusion.20
  251.7 3.9 %maximum_multiply_fusion = f32[32,2,128,256]{2,3,0,1:T(8,128)} fusion(f32[32,1,128,256]{2,3,0,1:T(8,128)S(1)} %fusion.18, f32[32,1,128,256]{2,3,0,1:T(8,128)S(1)} %fusion.20), kind=kLoop, calls=%fused_computation.53 | loop fusion | flops 4194304 | bytes 16777216 | tf_op jit(solution)/shard_map/mul | solution.py:142
  255.6 8.9 %copy.187 = f32[32,2,128,256]{3,2,1,0:T(8,128)} copy(f32[32,2,128,256]{2,3,0,1:T(8,128)} %maximum_multiply_fusion) | data formatting | bytes 16777216 | tf_op jit(solution)/shard_map/mul | solution.py:142
  (79 shorter events, 11.6 us)
Async XLA Ops:
  33.7 8.5 %copy-start.5 = (s32[1,4]{1,0:T(1,128)S(1)}, s32[1,4]{1,0:T(1,128)}, u32[]{:S(2)}) copy-start(s32[1,4]{1,0:T(1,128)} %param.9) | copy-start | bytes 52
  33.7 10.5 %copy-start.4 = (bf16[1,64,64]{2,1,0:T(8,128)(2,1)S(1)}, bf16[1,64,64]{2,1,0:T(8,128)(2,1)}, u32[]{:S(2)}) copy-start(bf16[1,64,64]{2,1,0:T(8,128)(2,1)} %param.8) | copy-start | bytes 24580
  33.7 73.2 %all-to-all-start = ((bf16[16,2,16384]{2,1,0:T(2,128)(2,1)}), bf16[16,2,16384]{2,1,0:T(2,128)(2,1)S(1)}, u32[]{:S(2)}, u32[]{:S(2)}) async-start(bf16[16,2,16384]{2,1,0:T(2,128)(2,1)} %reshape.572), calls=%async_computation | async-start | bytes 2097152 | tf_op jit(solution)/shard_map/all_to_all | solution.py:107
  42.3 52.6 %collective-permute-start = (s32[1,4]{0,1:T(4,128)S(1)}, s32[1,4]{0,1:T(4,128)S(1)}, u32[]{:S(2)}, u32[]{:S(2)}) collective-permute-start(s32[1,4]{0,1:T(4,128)S(1)} %copy.155), channel_id=1, source_target_pairs={{0,2},{2,0},{4,6},{6,4},{8,10},{10,8},{12,14},{14,12},{16,18},{18,... | collective-permute-start | bytes 56 | tf_op jit(solution)/shard_map/ppermute | solution.py:18
  94.9 3.6 %collective-permute-start.1 = (s32[2,4]{0,1:T(4,128)S(1)}, s32[2,4]{0,1:T(4,128)S(1)}, u32[]{:S(2)}, u32[]{:S(2)}) collective-permute-start(s32[2,4]{0,1:T(4,128)S(1)} %add_select_fusion.2), channel_id=1, source_target_pairs={{0,4},{2,6},{4,0},{6,2},{8,12},{10,14},{12,8},{14,10},{16,20},{18,... | collective-permute-start | bytes 104 | tf_op jit(solution)/shard_map/ppermute | solution.py:18
  98.6 3.6 %collective-permute-start.2 = (s32[4,4]{0,1:T(4,128)S(1)}, s32[4,4]{0,1:T(4,128)S(1)}, u32[]{:S(2)}, u32[]{:S(2)}) collective-permute-start(s32[4,4]{0,1:T(4,128)S(1)} %add_select_fusion.3), channel_id=1, source_target_pairs={{0,8},{2,10},{4,12},{6,14},{8,0},{10,2},{12,4},{14,6},{16,24},{18,... | collective-permute-start | bytes 200 | tf_op jit(solution)/shard_map/ppermute | solution.py:18
  102.3 4.5 %collective-permute-start.3 = (s32[8,4]{0,1:T(4,128)S(1)}, s32[8,4]{0,1:T(4,128)S(1)}, u32[]{:S(2)}, u32[]{:S(2)}) collective-permute-start(s32[8,4]{0,1:T(4,128)S(1)} %add_select_fusion.4), channel_id=1, source_target_pairs={{0,16},{2,18},{4,20},{6,22},{8,24},{10,26},{12,28},{14,30},{16,0},... | collective-permute-start | bytes 392 | tf_op jit(solution)/shard_map/ppermute | solution.py:18
  144.7 1.0 copy-start
  154.7 1.7 copy-start.1
  156.4 1.0 copy-start
  166.4 1.7 copy-start.1
  168.1 1.2 copy-start.2
  173.6 19.2 %all-to-all-start.1 = ((bf16[2,1,256,1024]{3,0,1,2:T(2,128)(2,1)}), bf16[2,1,256,1024]{3,0,1,2:T(2,128)(2,1)S(1)}, u32[]{:S(2)}, u32[]{:S(2)}) async-start(bf16[2,1,256,1024]{3,0,1,2:T(2,128)(2,1)} %copy.163), calls=%async_computation.1 | async-start | bytes 2097152 | tf_op jit(solution)/shard_map/all_to_all | solution.py:132
  177.3 68.8 %all-gather.2.cloned.1.call-start = ((), (), s32[]{:S(2)}) async-start(), calls=%async_computation.3 | async-start | bytes 3145728 | tf_op jit(solution)/shard_map/all_gather | solution.py:140
  198.5 1.2 copy-start.3
Sparse Core Ops, SparseCore 0:
  237.2 8.8 all-gather.1
